TPU v7x, 32 devices: a whole 2x2x4 slice. The times are simulated.
32 devices in a mesh: row: 8 (over z, x), col: 4 (over y, core).
Axes of the slice: x: 2, y: 2, z: 4, core: 2. Of those that a mesh axis runs over, the one named last changes fastest.
Arguments:
- tokens: bfloat16 [64, 512, 512], P('row', 'col'), may hold values from -6 to 6
- ln1_gain: float32 [512], replicated, may hold values from 0.1 to 1.9
- w_qkv: bfloat16 [512, 1536], replicated
- rel_bias: float32 [16, 49], replicated, may hold values from -4 to 4
- w_proj: bfloat16 [512, 512], replicated, may hold values from -0.25 to 0.25
- ln2_gain: float32 [512], replicated, may hold values from 0.1 to 1.9
- w_up: bfloat16 [512, 2048], replicated, may hold values from -0.25 to 0.25
- w_down: bfloat16 [2048, 512], replicated, may hold values from -0.125 to 0.125
- merge_gain: float32 [2048], replicated, may hold values from 0.3 to 3
- w_merge: bfloat16 [2048, 1024], replicated, may hold values from -0.125 to 0.125
- cotangent: bfloat16 [32, 256, 1024], P('row', 'col'), may hold values from -6 to 6
Outputs:
- merged: bfloat16 [32, 256, 1024], P('row', 'col')
- grad_merge: float32 [2048, 1024], P(('row', 'col'))
- grad_down: float32 [2048, 512], P(('row', 'col'))
All inputs are finite; a program needn't handle non-finite values.
Results may differ from a plain program's by a relative error of at most 0.012.
Values may be sent and summed in bfloat16 or wider, within the bound.
A program may use at most 128 MiB of HBM per device.

v0:
```python
import jax
import jax.numpy as jnp
from jax import lax
from jax.sharding import PartitionSpec as P


def with_halo(cells, sides, width):
    for axis, dim in sides:
        count = lax.axis_size(axis)
        ends = count - 1
        head = lax.slice_in_dim(cells, 0, width, axis=dim)
        tail = lax.slice_in_dim(cells, cells.shape[dim] - width, cells.shape[dim], axis=dim)
        cells = jnp.concatenate(
            [
                lax.ppermute(tail, axis, [(i, (i + 1) % count) for i in range(ends)]),
                cells,
                lax.ppermute(head, axis, [((i + 1) % count, i) for i in range(ends)]),
            ],
            axis=dim,
        )
    return cells


def layer_norm(value, gain):
    mean = jnp.mean(value, axis=-1, keepdims=True)
    var = jnp.mean((value - mean) ** 2, axis=-1, keepdims=True)
    return (value - mean) / jnp.sqrt(var + 1e-05) * gain


def local(
    tokens,
    ln1_gain,
    w_qkv,
    rel_bias,
    w_proj,
    ln2_gain,
    w_up,
    w_down,
    merge_gain,
    w_merge,
    cotangent,
):
    rows, cols, width = tokens.shape
    heads = rel_bias.shape[0]
    head_dim = width // heads
    x_flat = tokens.astype(jnp.float32).reshape(-1, width)
    normed = layer_norm(x_flat, ln1_gain).astype(jnp.bfloat16)
    query = jnp.dot(normed, w_qkv[:, :width], preferred_element_type=jnp.float32).astype(
        jnp.bfloat16
    )
    query_t = query.reshape(rows, cols, heads, head_dim).transpose(0, 2, 3, 1)
    keyval = jnp.dot(normed, w_qkv[:, width:], preferred_element_type=jnp.float32).astype(
        jnp.bfloat16
    )
    keyval = keyval.reshape(rows, cols, 2 * width).transpose(0, 2, 1)
    padded = with_halo(keyval, (("row", 0), ("col", 2)), 3)
    padded = padded.reshape(rows + 6, 2, heads, head_dim, cols + 6)
    total_rows = rows * lax.axis_size("row")
    total_cols = cols * lax.axis_size("col")
    row_pos = lax.axis_index("row") * rows + jnp.arange(rows)
    col_pos = lax.axis_index("col") * cols + jnp.arange(cols)
    scores = []
    masks = []
    for di in range(7):
        for dj in range(7):
            key = padded[di : di + rows, 0, :, :, dj : dj + cols]
            scores.append(
                jnp.einsum("rhdc,rhdc->rhc", query_t, key, preferred_element_type=jnp.float32)
            )
            rows_ok = (row_pos + di - 3 >= 0) & (row_pos + di - 3 < total_rows)
            cols_ok = (col_pos + dj - 3 >= 0) & (col_pos + dj - 3 < total_cols)
            masks.append(rows_ok[:, None] & cols_ok[None, :])
    scale = 1.0 / jnp.sqrt(jnp.float32(head_dim))
    score = jnp.stack(scores, 0) * scale + rel_bias.T[:, None, :, None]
    valid = jnp.stack(masks, 0)[:, :, None, :]
    score = jnp.where(valid, score, -1e30)
    top = jnp.max(score, axis=0, keepdims=True)
    expo = jnp.where(valid, jnp.exp(score - top), 0.0)
    probs = (expo / jnp.sum(expo, axis=0, keepdims=True)).astype(jnp.bfloat16)
    attn = jnp.zeros((rows, heads, head_dim, cols), jnp.float32)
    offset = 0
    for di in range(7):
        for dj in range(7):
            value = padded[di : di + rows, 1, :, :, dj : dj + cols]
            attn = attn + jnp.einsum(
                "rhc,rhdc->rhdc", probs[offset], value, preferred_element_type=jnp.float32
            )
            offset += 1
    attn = attn.astype(jnp.bfloat16).transpose(0, 3, 1, 2).reshape(-1, width)
    h_one = (x_flat + jnp.dot(attn, w_proj, preferred_element_type=jnp.float32)).astype(
        jnp.bfloat16
    )
    normed2 = layer_norm(h_one.astype(jnp.float32), ln2_gain).astype(jnp.bfloat16)
    hidden = jax.nn.gelu(
        jnp.dot(normed2, w_up, preferred_element_type=jnp.float32), approximate=False
    ).astype(jnp.bfloat16)
    out_y = (
        h_one.astype(jnp.float32) + jnp.dot(hidden, w_down, preferred_element_type=jnp.float32)
    ).astype(jnp.bfloat16)
    joined = (
        out_y.reshape(rows // 2, 2, cols // 2, 2, width)
        .transpose(0, 2, 3, 1, 4)
        .reshape(-1, 4 * width)
        .astype(jnp.float32)
    )
    mean = jnp.mean(joined, axis=-1, keepdims=True)
    inv = 1.0 / jnp.sqrt(jnp.mean((joined - mean) ** 2, axis=-1, keepdims=True) + 1e-05)
    unit = (joined - mean) * inv
    merge_in = (unit * merge_gain).astype(jnp.bfloat16)
    merged = jnp.dot(merge_in, w_merge, preferred_element_type=jnp.float32).astype(jnp.bfloat16)
    merged = merged.reshape(rows // 2, cols // 2, 2 * width)
    cot = cotangent.reshape(-1, 2 * width)
    grad_m = jnp.dot(merge_in.T, cot, preferred_element_type=jnp.float32)
    grad_n = jnp.dot(cot, w_merge.T, preferred_element_type=jnp.float32) * merge_gain
    grad_z = (
        grad_n
        - jnp.mean(grad_n, axis=-1, keepdims=True)
        - unit * jnp.mean(grad_n * unit, axis=-1, keepdims=True)
    ) * inv
    grad_y = (
        grad_z.astype(jnp.bfloat16)
        .reshape(rows // 2, cols // 2, 2, 2, width)
        .transpose(0, 3, 1, 2, 4)
        .reshape(-1, width)
    )
    grad_d = jnp.dot(hidden.T, grad_y, preferred_element_type=jnp.float32)
    count = grad_m.size + grad_d.size
    sum_m, sum_d = lax.psum((grad_m, grad_d), ("row", "col"))
    total = jnp.sum(sum_m * sum_m) + jnp.sum(sum_d * sum_d)
    groups = lax.axis_size(("row", "col"))
    index = lax.axis_index(("row", "col"))
    share_m = lax.dynamic_slice_in_dim(
        sum_m, index * (sum_m.shape[0] // groups), sum_m.shape[0] // groups, 0
    )
    share_d = lax.dynamic_slice_in_dim(
        sum_d, index * (sum_d.shape[0] // groups), sum_d.shape[0] // groups, 0
    )
    factor = 1.0 / jnp.sqrt(total / count + 1e-06)
    return (merged, share_m * factor, share_d * factor)


def solution(mesh):
    placed = (
        P("row", "col", None),
        P(),
        P(),
        P(),
        P(),
        P(),
        P(),
        P(),
        P(),
        P(),
        P("row", "col", None),
    )
    return jax.shard_map(
        local,
        mesh=mesh,
        in_specs=placed,
        out_specs=(P("row", "col", None), P(("row", "col"), None), P(("row", "col"), None)),
        check_vma=False,
    )
```

profile of v0, /device:TPU:0, one launch (start us, length us, event | category | flops | bytes accessed | tf_op | source)
XLA Modules:
  0.0 520.5 jit_solution(10870981523958563618)
XLA Ops:
  7.3 1.6 convert_reduce_fusion.1
  8.9 1.7 fusion.116
  11.1 2.6 convolution_convert_fusion
  13.7 3.9 copy.119
  17.6 2.6 fusion.141
  20.2 5.8 %collective-permute-start = (bf16[3,1024,128]{2,1,0:T(8,128)(2,1)}, bf16[3,1024,128]{2,1,0:T(8,128)(2,1)}, u32[]{:S(2)}, u32[]{:S(2)}) collective-permute-start(bf16[3,1024,128]{2,1,0:T(8,128)(2,1)} %get-tuple-element.58), channel_id=1, source_target_pairs={{0,4},{4,8},{8,12},{12,16},{16,20},{20,24},{24,28},{1,5},{5,9},{9,... | collective-permute-start | bytes 2359304 | tf_op jit(solution)/shard_map/ppermute | solution.py:15
  26.0 1.3 collective-permute-start.1
  27.4 3.1 convolution_convert_fusion.1
  34.1 2.3 copy.118
  36.4 1.5 copy.518
  38.1 1.6 bitcast_convert_fusion
  39.6 19.4 %collective-permute-done = bf16[3,1024,128]{2,1,0:T(8,128)(2,1)} collective-permute-done((bf16[3,1024,128]{2,1,0:T(8,128)(2,1)}, bf16[3,1024,128]{2,1,0:T(8,128)(2,1)}, u32[]{:S(2)}, u32[]{:S(2)}) %collective-permute-start) | collective-permute-done | bytes 786464 | tf_op jit(solution)/shard_map/ppermute | solution.py:15
  59.0 1.6 pad_maximum_fusion.1
  60.6 4.3 fusion.140
  64.9 3.7 copy.120
  68.6 3.7 copy.121
  72.3 1.3 collective-permute-start.3
  73.6 3.8 collective-permute-start.2
  78.2 3.9 copy.122
  82.1 3.1 copy.123
  85.2 8.4 %pad_maximum_fusion = bf16[14,1024,134]{2,1,0:T(8,128)(2,1)S(1)} fusion(bf16[14,1024,3]{2,1,0:T(8,128)(2,1)} %copy.123, bf16[3,1024,128]{2,1,0:T(8,128)(2,1)} %collective-permute-done.1, bf16[8,1024,128]{2,1,0:T(8,128)(2,1)} %bitcast.1631, bf16[3,1024,128]{2,1,0:T(8,128)(2,1)} %collective-permute-done, bf16[14,1024,3]{2,1,0:T(8,128)(2,1)} %copy.122), kind=kLoop, calls=%fused_computation.20 | loop fusion | flops 19210240 | bytes 7684096 | tf_op jit(solution)/shard_map/concatenate | solution.py:13
  93.6 7.9 %multiply_reduce_fusion.38 = (f32[8,16,128]{2,1,0:T(8,128)}, f32[8,16,128]{2,1,0:T(8,128)}, f32[8,16,128]{2,1,0:T(8,128)}, f32[8,16,128]{2,1,0:T(8,128)}, f32[8,...) fusion(bf16[14,2,16,32,134]{4,3,2,1,0:T(8,128)(2,1)S(1)} %bitca, ...), kind=kLoop, calls=%fused_computation.230 | loop fusion | flops 20234240 | bytes 16580608 | tf_op jit(solution)/shard_map/rhdc,rhdc->rhc/dot_general | solution.py:68
  101.5 12.3 %multiply_reduce_fusion.20 = (f32[8,16,128]{2,1,0:T(8,128)}, f32[8,16,128]{2,1,0:T(8,128)}, f32[8,16,128]{2,1,0:T(8,128)}, f32[8,16,128]{2,1,0:T(8,128)}, f32[8,...) fusion(bf16[14,2,16,32,134]{4,3,2,1,0:T(8,128)(2,1)S(1)} %bitca, ...), kind=kLoop, calls=%fused_computation.212 | loop fusion | flops 28016640 | bytes 22151168 | tf_op jit(solution)/shard_map/rhdc,rhdc->rhc/dot_general | solution.py:68
  113.8 11.8 %multiply_reduce_fusion.2 = (f32[8,16,128]{2,1,0:T(8,128)S(1)}, f32[8,16,128]{2,1,0:T(8,128)S(1)}, f32[8,16,128]{2,1,0:T(8,128)S(1)}, f32[8,16,128]{2,1,0:T(8,12...) fusion(bf16[14,2,16,32,134]{4,3,2,1,0:T(8,128)(2,1)S(1)} %bitca, ...), kind=kLoop, calls=%fused_computation.194 | loop fusion | flops 28016640 | bytes 22151168 | tf_op jit(solution)/shard_map/rhdc,rhdc->rhc/dot_general | solution.py:68
  125.7 1.0 constant_dynamic-update-slice_fusion.97
  126.7 0.9 constant_dynamic-update-slice_fusion.96
  127.6 0.9 constant_dynamic-update-slice_fusion.95
  128.5 0.8 constant_dynamic-update-slice_fusion.94
  129.3 0.8 constant_dynamic-update-slice_fusion.93
  131.9 0.8 constant_dynamic-update-slice_fusion.90
  132.7 0.8 constant_dynamic-update-slice_fusion.89
  133.5 0.8 constant_dynamic-update-slice_fusion.88
  136.9 0.8 constant_dynamic-update-slice_fusion.84
  137.8 0.8 constant_dynamic-update-slice_fusion.83
  138.6 0.8 constant_dynamic-update-slice_fusion.82
  140.8 1.1 fusion.121
  141.8 1.3 divide_convert_fusion
  143.9 1.0 convert_bitcast_fusion.96
  144.9 1.0 convert_bitcast_fusion.97
  146.0 43.3 %fusion.19 = bf16[8,128,16,32]{1,3,2,0:T(8,128)(2,1)} fusion(bf16[14,2,16,32,134]{4,3,2,1,0:T(8,128)(2,1)} %bitcast.1629, f32[8,128,16]{1,2,0:T(8,128)} %get-tuple-element.61, f32[8,128,16]{1,2,0:T(8,128)} %get-tuple-element.62, f32[8,128,16]{1,2,0:T(8,128)} %get-tuple-element.63, f32[8,128,16]{1,2,0:T(8,128)} %get-tuple-element.64, ...), kind=kLoop, calls=%fused_computation.40 | loop fusion | flops 77070336 | bytes 55640064 | tf_op jit(solution)/shard_map/convert_element_type | solution.py:89
  189.3 2.0 copy.173
  192.7 20.9 %fusion.2 = bf16[1024,2048]{1,0:T(8,128)(2,1)S(1)} fusion(bf16[512,2048]{1,0:T(8,128)(2,1)S(1)} %copy-done, bf16[1024,512]{1,0:T(8,128)(2,1)S(1)} %get-tuple-element.112, f32[512]{0:T(512)S(1)} %copy-done.35, f32[1024]{0:T(1024)S(1)} %add_sqrt_fusion, f32[1024]{0:T(1024)S(1)} %broadcast_multiply_fusion), kind=kOutput, calls=%fused_computation.3 | convolution fusion | flops 2286419968 | bytes 7350272 | tf_op jit(solution)/shard_map/dot_general | solution.py:95
  213.6 1.9 copy-done.36
  215.5 3.7 fusion.122
  219.1 2.5 reshape.2795
  221.6 1.8 fusion.138
  223.5 4.1 multiply_reduce_fusion.52
  227.7 2.9 copy.583
  230.7 2.6 multiply_convert_fusion.1
  233.3 3.1 reshape.2695
  236.4 1.8 convert_element_type.87
  238.3 3.9 fusion.139
  242.2 1.7 multiply_convert_fusion
  244.0 2.6 reshape.2693
  246.6 3.0 copy.584
  249.6 2.5 reshape.2694
  252.1 6.8 %fusion.143 = f32[2048,512]{1,0:T(8,128)} fusion(bf16[1024,2048]{1,0:T(8,128)(2,1)} %copy-done.36, bf16[1024,512]{1,0:T(8,128)(2,1)} %reshape.2694), kind=kOutput, calls=%fused_computation.594 | convolution fusion | flops 2147483648 | bytes 9437184 | tf_op jit(solution)/shard_map/dot_general | solution.py:126
  259.0 4.5 fusion.142
  263.5 4.3 convolution_convert_fusion.2
  267.8 230.9 %all-reduce.3.cloned.1.call-done = (f32[2048,1024]{1,0:T(8,128)}, f32[2048,512]{1,0:T(8,128)}) async-done(((f32[2048,1024]{1,0:T(8,128)}, f32[2048,512]{1,0:T(8,128)}), (f32[2048,1024]{1,0:T(8,128)}, f32[2048,512]{1,0:T(8,128)})) %all-reduce.3.cloned.1.call-update) | async-done | bytes 12582928 | tf_op jit(solution)/shard_map/psum | solution.py:128
  498.7 3.9 multiply_reduce_fusion.1
  502.6 6.3 %multiply_reduce_fusion = f32[]{:T(128)} fusion(f32[2048,1024]{1,0:T(8,128)} %get-tuple-element.54), kind=kLoop, calls=%fused_computation.4 | loop fusion | flops 4194303 | bytes 8388612 | tf_op jit(solution)/shard_map/reduce_sum | solution.py:129
  510.2 1.7 dynamic-slice_multiply_fusion
  511.9 1.6 dynamic-slice_multiply_fusion.1
  (190 shorter events, 12.7 us)
Async XLA Ops:
  7.2 185.5 %copy-start = (bf16[512,2048]{1,0:T(8,128)(2,1)S(1)}, bf16[512,2048]{1,0:T(8,128)(2,1)}, u32[]{:S(2)}) copy-start(bf16[512,2048]{1,0:T(8,128)(2,1)} %param.17) | copy-start | bytes 6291460
  7.2 3.4 copy-start.5
  7.2 3.4 copy-start.31
  7.2 491.5 %all-reduce.3.cloned.1.call-start = ((), (), s32[]{:S(2)}) async-start(), calls=%async_computation | async-start | bytes 25165824 | tf_op jit(solution)/shard_map/psum | solution.py:128
  7.2 3.8 copy-start.33
  11.0 2.6 copy-start.7
  20.2 38.8 %collective-permute-start = (bf16[3,1024,128]{2,1,0:T(8,128)(2,1)}, bf16[3,1024,128]{2,1,0:T(8,128)(2,1)}, u32[]{:S(2)}, u32[]{:S(2)}) collective-permute-start(bf16[3,1024,128]{2,1,0:T(8,128)(2,1)} %get-tuple-element.58), channel_id=1, source_target_pairs={{0,4},{4,8},{8,12},{12,16},{16,20},{20,24},{24,28},{1,5},{5,9},{9,... | collective-permute-start | bytes 2359304 | tf_op jit(solution)/shard_map/ppermute | solution.py:15
  26.0 33.1 %collective-permute-start.1 = (bf16[3,1024,128]{2,1,0:T(8,128)(2,1)}, bf16[3,1024,128]{2,1,0:T(8,128)(2,1)}, u32[]{:S(2)}, u32[]{:S(2)}) collective-permute-start(bf16[3,1024,128]{2,1,0:T(8,128)(2,1)} %get-tuple-element.59), channel_id=1, source_target_pairs={{4,0},{8,4},{12,8},{16,12},{20,16},{24,20},{28,24},{5,1},{9,5},{13... | collective-permute-start | bytes 2359304 | tf_op jit(solution)/shard_map/ppermute | solution.py:17
  37.9 21.1 %copy-start.4 = (bf16[8,128,1024]{1,2,0:T(8,128)(2,1)S(1)}, bf16[8,128,1024]{1,2,0:T(8,128)(2,1)}, u32[]{:S(2)}) copy-start(bf16[8,128,1024]{1,2,0:T(8,128)(2,1)} %copy.119) | copy-start | bytes 6291460
  68.6 8.9 %copy-start.27 = (f32[2048]{0:T(1024)S(1)}, f32[2048]{0:T(1024)}, u32[]{:S(2)}) copy-start(f32[2048]{0:T(1024)} %param.19) | copy-start | bytes 24580
  68.6 9.5 %copy-start.30 = (f32[16,49]{1,0:T(8,128)S(1)}, f32[16,49]{1,0:T(8,128)}, u32[]{:S(2)}) copy-start(f32[16,49]{1,0:T(8,128)} %param.14) | copy-start | bytes 9412
  72.3 9.8 %collective-permute-start.3 = (bf16[14,1024,3]{1,0,2:T(8,128)(2,1)S(1)}, bf16[14,1024,3]{1,0,2:T(8,128)(2,1)S(1)}, u32[]{:S(2)}, u32[]{:S(2)}) collective-permute-start(bf16[14,1024,3]{1,0,2:T(8,128)(2,1)S(1)} %copy.121), channel_id=1, source_target_pairs={{1,0},{2,1},{3,2},{5,4},{6,5},{7,6},{9,8},{10,9},{11,10},{13,12},{... | collective-permute-start | bytes 258056 | tf_op jit(solution)/shard_map/ppermute | solution.py:17
  73.6 4.6 collective-permute-start.2
  85.2 8.4 %copy-start.3 = (f32[8,16,128,32]{2,0,3,1:T(8,128)S(1)}, f32[8,16,128,32]{2,0,3,1:T(8,128)}, u32[]{:S(2)}) copy-start(f32[8,16,128,32]{2,0,3,1:T(8,128)} %bitcast_convert_fusion) | copy-start | bytes 6291460
  93.6 20.2 %copy-start.2 = (bf16[14,1024,134]{2,1,0:T(8,128)(2,1)}, bf16[14,1024,134]{2,1,0:T(8,128)(2,1)S(1)}, u32[]{:S(2)}) copy-start(bf16[14,1024,134]{2,1,0:T(8,128)(2,1)S(1)} %pad_maximum_fusion) | copy-start | bytes 11526148
  125.6 13.9 %copy-start.26 = (f32[8,16,128]{2,1,0:T(8,128)S(1)}, f32[8,16,128]{2,1,0:T(8,128)}, u32[]{:S(2)}) copy-start(f32[8,16,128]{2,1,0:T(8,128)} %get-tuple-element.35) | copy-start | bytes 196612
  125.6 13.9 %copy-start.25 = (f32[8,16,128]{2,1,0:T(8,128)S(1)}, f32[8,16,128]{2,1,0:T(8,128)}, u32[]{:S(2)}) copy-start(f32[8,16,128]{2,1,0:T(8,128)} %get-tuple-element.34) | copy-start | bytes 196612
  125.6 13.9 %copy-start.24 = (f32[8,16,128]{2,1,0:T(8,128)S(1)}, f32[8,16,128]{2,1,0:T(8,128)}, u32[]{:S(2)}) copy-start(f32[8,16,128]{2,1,0:T(8,128)} %get-tuple-element.33) | copy-start | bytes 196612
  125.6 13.9 %copy-start.23 = (f32[8,16,128]{2,1,0:T(8,128)S(1)}, f32[8,16,128]{2,1,0:T(8,128)}, u32[]{:S(2)}) copy-start(f32[8,16,128]{2,1,0:T(8,128)} %get-tuple-element.32) | copy-start | bytes 196612
  125.6 14.0 %copy-start.22 = (f32[8,16,128]{2,1,0:T(8,128)S(1)}, f32[8,16,128]{2,1,0:T(8,128)}, u32[]{:S(2)}) copy-start(f32[8,16,128]{2,1,0:T(8,128)} %get-tuple-element.31) | copy-start | bytes 196612
  125.6 14.0 %copy-start.21 = (f32[8,16,128]{2,1,0:T(8,128)S(1)}, f32[8,16,128]{2,1,0:T(8,128)}, u32[]{:S(2)}) copy-start(f32[8,16,128]{2,1,0:T(8,128)} %get-tuple-element.30) | copy-start | bytes 196612
  125.6 14.0 %copy-start.20 = (f32[8,16,128]{2,1,0:T(8,128)S(1)}, f32[8,16,128]{2,1,0:T(8,128)}, u32[]{:S(2)}) copy-start(f32[8,16,128]{2,1,0:T(8,128)} %get-tuple-element.29) | copy-start | bytes 196612
  125.6 14.0 %copy-start.19 = (f32[8,16,128]{2,1,0:T(8,128)S(1)}, f32[8,16,128]{2,1,0:T(8,128)}, u32[]{:S(2)}) copy-start(f32[8,16,128]{2,1,0:T(8,128)} %get-tuple-element.28) | copy-start | bytes 196612
  125.6 14.0 %copy-start.18 = (f32[8,16,128]{2,1,0:T(8,128)S(1)}, f32[8,16,128]{2,1,0:T(8,128)}, u32[]{:S(2)}) copy-start(f32[8,16,128]{2,1,0:T(8,128)} %get-tuple-element.27) | copy-start | bytes 196612
  125.6 14.0 %copy-start.17 = (f32[8,16,128]{2,1,0:T(8,128)S(1)}, f32[8,16,128]{2,1,0:T(8,128)}, u32[]{:S(2)}) copy-start(f32[8,16,128]{2,1,0:T(8,128)} %get-tuple-element.26) | copy-start | bytes 196612
  125.6 14.0 %copy-start.16 = (f32[8,16,128]{2,1,0:T(8,128)S(1)}, f32[8,16,128]{2,1,0:T(8,128)}, u32[]{:S(2)}) copy-start(f32[8,16,128]{2,1,0:T(8,128)} %get-tuple-element.25) | copy-start | bytes 196612
  125.7 14.1 %copy-start.15 = (f32[8,16,128]{2,1,0:T(8,128)S(1)}, f32[8,16,128]{2,1,0:T(8,128)}, u32[]{:S(2)}) copy-start(f32[8,16,128]{2,1,0:T(8,128)} %get-tuple-element.24) | copy-start | bytes 196612
  125.7 14.1 %copy-start.14 = (f32[8,16,128]{2,1,0:T(8,128)S(1)}, f32[8,16,128]{2,1,0:T(8,128)}, u32[]{:S(2)}) copy-start(f32[8,16,128]{2,1,0:T(8,128)} %get-tuple-element.23) | copy-start | bytes 196612
  125.7 14.1 %copy-start.13 = (f32[8,16,128]{2,1,0:T(8,128)S(1)}, f32[8,16,128]{2,1,0:T(8,128)}, u32[]{:S(2)}) copy-start(f32[8,16,128]{2,1,0:T(8,128)} %get-tuple-element.22) | copy-start | bytes 196612
  125.7 14.1 %copy-start.12 = (f32[8,16,128]{2,1,0:T(8,128)S(1)}, f32[8,16,128]{2,1,0:T(8,128)}, u32[]{:S(2)}) copy-start(f32[8,16,128]{2,1,0:T(8,128)} %get-tuple-element.21) | copy-start | bytes 196612
  125.7 14.1 %copy-start.11 = (f32[8,16,128]{2,1,0:T(8,128)S(1)}, f32[8,16,128]{2,1,0:T(8,128)}, u32[]{:S(2)}) copy-start(f32[8,16,128]{2,1,0:T(8,128)} %get-tuple-element.20) | copy-start | bytes 196612
  125.7 14.1 %copy-start.10 = (f32[8,16,128]{2,1,0:T(8,128)S(1)}, f32[8,16,128]{2,1,0:T(8,128)}, u32[]{:S(2)}) copy-start(f32[8,16,128]{2,1,0:T(8,128)} %get-tuple-element.19) | copy-start | bytes 196612
  126.7 13.1 %copy-start.9 = (f32[8,16,128]{2,1,0:T(8,128)S(1)}, f32[8,16,128]{2,1,0:T(8,128)}, u32[]{:S(2)}) copy-start(f32[8,16,128]{2,1,0:T(8,128)} %get-tuple-element.18) | copy-start | bytes 196612
  127.6 12.3 %copy-start.8 = (f32[8,16,128]{2,1,0:T(8,128)S(1)}, f32[8,16,128]{2,1,0:T(8,128)}, u32[]{:S(2)}) copy-start(f32[8,16,128]{2,1,0:T(8,128)} %get-tuple-element.17) | copy-start | bytes 196612
  189.2 2.0 copy-start.34
  191.2 1.4 copy-start.35
  192.6 22.8 %copy-start.32 = (bf16[2048,512]{1,0:T(8,128)(2,1)S(1)}, bf16[2048,512]{1,0:T(8,128)(2,1)}, u32[]{:S(2)}) copy-start(bf16[2048,512]{1,0:T(8,128)(2,1)} %param.18) | copy-start | bytes 6291460
  213.5 1.9 copy-start.36
  227.6 3.1 copy-start.29
  236.4 1.9 copy-start.28
  252.1 6.9 %copy-start.6 = (bf16[4,64,1024]{2,1,0:T(8,128)(2,1)S(1)}, bf16[4,64,1024]{2,1,0:T(8,128)(2,1)}, u32[]{:S(2)}) copy-start(bf16[4,64,1024]{2,1,0:T(8,128)(2,1)} %param.21) | copy-start | bytes 1572868
  502.6 10.9 %copy-start.1 = (bf16[512,2048]{1,0:T(8,128)(2,1)S(1)}, bf16[512,2048]{1,0:T(8,128)(2,1)}, u32[]{:S(2)}) copy-start(bf16[512,2048]{1,0:T(8,128)(2,1)} %param.17) | copy-start | bytes 6291460
Sparse Core Ops, SparseCore 0:
  263.6 235.0 all-reduce.2
where the time goes:
time: 527 us; the launch traced here: 521 us
  waiting for transfers between devices  250 us (47%)
  other arithmetic  125 us (24%)
  local copies, waits for them, and re-layouts  66.3 us (13%)
  matrix products  50.6 us (10%)
  between operations  16.6 us (3%)
  starting transfers between devices  12.2 us (2%)
    psum x1, waiting for transfers between devices, local(): sum_m, sum_d = lax.psum((grad_m, grad_d), ('row', 'col'))  231 us
    convert_element_type x1, other arithmetic, local(): attn = attn.astype(jnp.bfloat16).transpose(0, 3, 1, 2).reshape(-1, width)  43.3 us
    dot_general x3, other arithmetic, local(): jnp.einsum('rhdc,rhdc->rhc', query_t, key, preferred_element_type=jnp.flo...  31.9 us
    dot_general x1, matrix products, local(): jnp.dot(normed2, w_up, preferred_element_type=jnp.float32)  20.9 us
    ppermute x2, waiting for transfers between devices, with_halo(): lax.ppermute(tail, axis, [(i, (i + 1) % count) for i in range(ends)])  19.4 us
    unnamed x123, local copies, waits for them, and re-layouts  17.5 us
    slice x3, local copies, waits for them, and re-layouts, with_halo(): lax.slice_in_dim(cells, cells.shape[dim] - width, cells.shape[dim], axis=...  10.6 us
  transfers between devices with their start and end apart: 5, of which 2 were waited for; matrix products, arithmetic and copies ran while one was open for 4% of the time, Pallas kernels for 0%

commit v1 on v0

--- a/solution.py
+++ b/solution.py
@@ -2,6 +2,7 @@
 import jax.numpy as jnp
 from jax import lax
 from jax.sharding import PartitionSpec as P
+from jax.lax import psum
 
 
 def with_halo(cells, sides, width):
@@ -125,7 +126,7 @@
     )
     grad_d = jnp.dot(hidden.T, grad_y, preferred_element_type=jnp.float32)
     count = grad_m.size + grad_d.size
-    sum_m, sum_d = lax.psum((grad_m, grad_d), ("row", "col"))
+    sum_m, sum_d = psum(psum((grad_m, grad_d), "row"), "col")
     total = jnp.sum(sum_m * sum_m) + jnp.sum(sum_d * sum_d)
     groups = lax.axis_size(("row", "col"))
     index = lax.axis_index(("row", "col"))

time: 527 us -> 914 us (1.73)
  waiting for transfers between devices: 250 us -> 636 us
    psum x1 -> x2, waiting for transfers between devices: 231 us -> 617 us  [local(): sum_m, sum_d = psum(psum((grad_m, grad_d), 'row'), 'col')]
  transfers between devices with their start and end apart: 5 -> 6, of which waited for: 2 -> 3; matrix products, arithmetic and copies ran while one was open for 4% -> 2% of each run, Pallas kernels for 0% -> 0%
where the time goes in v1:
time: 914 us; the launch traced here: 907 us
  waiting for transfers between devices  636 us (70%)
  other arithmetic  125 us (14%)
  local copies, waits for them, and re-layouts  66.1 us (7%)
  matrix products  50.6 us (6%)
  between operations  16.6 us (2%)
  starting transfers between devices  12.5 us (1%)
    psum x2, waiting for transfers between devices, local(): sum_m, sum_d = psum(psum((grad_m, grad_d), 'row'), 'col')  617 us
    convert_element_type x1, other arithmetic, local(): attn = attn.astype(jnp.bfloat16).transpose(0, 3, 1, 2).reshape(-1, width)  43.3 us
    dot_general x3, other arithmetic, local(): jnp.einsum('rhdc,rhdc->rhc', query_t, key, preferred_element_type=jnp.flo...  31.9 us
    dot_general x1, matrix products, local(): jnp.dot(normed2, w_up, preferred_element_type=jnp.float32)  20.9 us
    ppermute x2, waiting for transfers between devices, with_halo(): lax.ppermute(tail, axis, [(i, (i + 1) % count) for i in range(ends)])  19.4 us
  transfers between devices with their start and end apart: 6, of which 3 were waited for; matrix products, arithmetic and copies ran while one was open for 2% of the time, Pallas kernels for 0%

profile of v1, /device:TPU:0, one launch (start us, length us, event | category | flops | bytes accessed | tf_op | source)
XLA Modules:
  0.0 906.7 jit_solution(2606089179599154916)
XLA Ops:
  7.3 1.6 convert_reduce_fusion.1
  8.9 1.7 fusion.116
  11.1 2.6 convolution_convert_fusion
  13.7 3.9 copy.119
  17.6 2.6 fusion.141
  20.2 5.8 collective-permute-start
  26.0 1.3 collective-permute-start.1
  27.4 3.1 convolution_convert_fusion.1
  34.1 2.3 copy.118
  36.4 1.5 copy.518
  38.1 1.6 bitcast_convert_fusion
  39.6 19.4 %collective-permute-done = bf16[3,1024,128]{2,1,0:T(8,128)(2,1)} collective-permute-done((bf16[3,1024,128]{2,1,0:T(8,128)(2,1)}, bf16[3,1024,128]{2,1,0:T(8,128)(2,1)}, u32[]{:S(2)}, u32[]{:S(2)}) %collective-permute-start) | collective-permute-done | bytes 786464 | tf_op jit(solution)/shard_map/ppermute | solution.py:16
  59.0 1.6 pad_maximum_fusion.1
  60.6 4.3 fusion.140
  64.9 3.7 copy.120
  68.6 3.7 copy.121
  72.3 1.3 collective-permute-start.3
  73.6 3.8 collective-permute-start.2
  78.2 3.9 copy.122
  82.1 3.1 copy.123
  85.2 8.4 pad_maximum_fusion
  93.6 7.9 multiply_reduce_fusion.38
  101.5 12.3 %multiply_reduce_fusion.20 = (f32[8,16,128]{2,1,0:T(8,128)}, f32[8,16,128]{2,1,0:T(8,128)}, f32[8,16,128]{2,1,0:T(8,128)}, f32[8,16,128]{2,1,0:T(8,128)}, f32[8,...) fusion(bf16[14,2,16,32,134]{4,3,2,1,0:T(8,128)(2,1)S(1)} %bitca, ...), kind=kLoop, calls=%fused_computation.212 | loop fusion | flops 28016640 | bytes 22151168 | tf_op jit(solution)/shard_map/rhdc,rhdc->rhc/dot_general | solution.py:69
  113.8 11.8 %multiply_reduce_fusion.2 = (f32[8,16,128]{2,1,0:T(8,128)S(1)}, f32[8,16,128]{2,1,0:T(8,128)S(1)}, f32[8,16,128]{2,1,0:T(8,128)S(1)}, f32[8,16,128]{2,1,0:T(8,12...) fusion(bf16[14,2,16,32,134]{4,3,2,1,0:T(8,128)(2,1)S(1)} %bitca, ...), kind=kLoop, calls=%fused_computation.194 | loop fusion | flops 28016640 | bytes 22151168 | tf_op jit(solution)/shard_map/rhdc,rhdc->rhc/dot_general | solution.py:69
  125.7 1.0 constant_dynamic-update-slice_fusion.97
  126.7 0.9 constant_dynamic-update-slice_fusion.96
  127.6 0.9 constant_dynamic-update-slice_fusion.95
  128.5 0.8 constant_dynamic-update-slice_fusion.94
  131.9 0.8 constant_dynamic-update-slice_fusion.90
  132.7 0.8 constant_dynamic-update-slice_fusion.89
  133.5 0.8 constant_dynamic-update-slice_fusion.88
  136.9 0.8 constant_dynamic-update-slice_fusion.84
  137.8 0.8 constant_dynamic-update-slice_fusion.83
  138.6 0.8 constant_dynamic-update-slice_fusion.82
  140.8 1.1 fusion.121
  141.8 1.3 divide_convert_fusion
  143.9 1.0 convert_bitcast_fusion.96
  144.9 1.0 convert_bitcast_fusion.97
  146.0 43.3 %fusion.19 = bf16[8,128,16,32]{1,3,2,0:T(8,128)(2,1)} fusion(bf16[14,2,16,32,134]{4,3,2,1,0:T(8,128)(2,1)} %bitcast.1629, f32[8,128,16]{1,2,0:T(8,128)} %get-tuple-element.63, f32[8,128,16]{1,2,0:T(8,128)} %get-tuple-element.64, f32[8,128,16]{1,2,0:T(8,128)} %get-tuple-element.65, f32[8,128,16]{1,2,0:T(8,128)} %get-tuple-element.66, ...), kind=kLoop, calls=%fused_computation.40 | loop fusion | flops 77070336 | bytes 55640064 | tf_op jit(solution)/shard_map/convert_element_type | solution.py:90
  189.3 2.0 copy.173
  192.7 20.9 %fusion.2 = bf16[1024,2048]{1,0:T(8,128)(2,1)S(1)} fusion(bf16[512,2048]{1,0:T(8,128)(2,1)S(1)} %copy-done, bf16[1024,512]{1,0:T(8,128)(2,1)S(1)} %get-tuple-element.114, f32[512]{0:T(512)S(1)} %copy-done.35, f32[1024]{0:T(1024)S(1)} %add_sqrt_fusion, f32[1024]{0:T(1024)S(1)} %broadcast_multiply_fusion), kind=kOutput, calls=%fused_computation.3 | convolution fusion | flops 2286419968 | bytes 7350272 | tf_op jit(solution)/shard_map/dot_general | solution.py:96
  213.6 1.9 copy-done.36
  215.5 3.7 fusion.122
  219.1 2.5 reshape.2795
  221.6 1.8 fusion.138
  223.5 4.1 multiply_reduce_fusion.52
  227.7 2.9 copy.583
  230.7 2.6 multiply_convert_fusion.1
  233.3 3.1 reshape.2695
  236.4 1.8 convert_element_type.87
  238.3 3.9 fusion.139
  242.2 1.7 multiply_convert_fusion
  244.0 2.6 reshape.2693
  246.6 3.0 copy.584
  249.6 2.3 reshape.2694
  251.9 6.9 fusion.143
  258.8 4.5 fusion.142
  263.6 398.8 %all-reduce.5.cloned.1.call-done = (f32[2048,1024]{1,0:T(8,128)}, f32[2048,512]{1,0:T(8,128)}) async-done(((f32[2048,1024]{1,0:T(8,128)}, f32[2048,512]{1,0:T(8,128)}), (f32[2048,1024]{1,0:T(8,128)}, f32[2048,512]{1,0:T(8,128)})) %all-reduce.5.cloned.1.call-update) | async-done | bytes 12582928 | tf_op jit(solution)/shard_map/psum | solution.py:129
  662.4 4.3 convolution_convert_fusion.2
  666.7 218.2 %all-reduce.7.cloned.1.call-done = (f32[2048,1024]{1,0:T(8,128)}, f32[2048,512]{1,0:T(8,128)}) async-done(((f32[2048,1024]{1,0:T(8,128)}, f32[2048,512]{1,0:T(8,128)}), (f32[2048,1024]{1,0:T(8,128)}, f32[2048,512]{1,0:T(8,128)})) %all-reduce.7.cloned.1.call-update) | async-done | bytes 12582928 | tf_op jit(solution)/shard_map/psum | solution.py:129
  884.8 3.9 multiply_reduce_fusion.1
  888.7 6.3 multiply_reduce_fusion
  896.3 1.7 dynamic-slice_multiply_fusion
  898.0 1.6 dynamic-slice_multiply_fusion.1
  (193 shorter events, 13.8 us)
Async XLA Ops:
  7.2 185.5 %copy-start = (bf16[512,2048]{1,0:T(8,128)(2,1)S(1)}, bf16[512,2048]{1,0:T(8,128)(2,1)}, u32[]{:S(2)}) copy-start(bf16[512,2048]{1,0:T(8,128)(2,1)} %param.17) | copy-start | bytes 6291460
  7.2 3.4 copy-start.5
  7.2 3.4 copy-start.31
  7.2 655.1 %all-reduce.5.cloned.1.call-start = ((), (), s32[]{:S(2)}) async-start(), calls=%async_computation | async-start | bytes 25165824 | tf_op jit(solution)/shard_map/psum | solution.py:129
  7.2 3.8 copy-start.33
  11.0 2.6 copy-start.7
  20.2 38.8 %collective-permute-start = (bf16[3,1024,128]{2,1,0:T(8,128)(2,1)}, bf16[3,1024,128]{2,1,0:T(8,128)(2,1)}, u32[]{:S(2)}, u32[]{:S(2)}) collective-permute-start(bf16[3,1024,128]{2,1,0:T(8,128)(2,1)} %get-tuple-element.60), channel_id=1, source_target_pairs={{0,4},{4,8},{8,12},{12,16},{16,20},{20,24},{24,28},{1,5},{5,9},{9,... | collective-permute-start | bytes 2359304 | tf_op jit(solution)/shard_map/ppermute | solution.py:16
  26.0 33.1 %collective-permute-start.1 = (bf16[3,1024,128]{2,1,0:T(8,128)(2,1)}, bf16[3,1024,128]{2,1,0:T(8,128)(2,1)}, u32[]{:S(2)}, u32[]{:S(2)}) collective-permute-start(bf16[3,1024,128]{2,1,0:T(8,128)(2,1)} %get-tuple-element.61), channel_id=1, source_target_pairs={{4,0},{8,4},{12,8},{16,12},{20,16},{24,20},{28,24},{5,1},{9,5},{13... | collective-permute-start | bytes 2359304 | tf_op jit(solution)/shard_map/ppermute | solution.py:18
  37.9 21.1 %copy-start.4 = (bf16[8,128,1024]{1,2,0:T(8,128)(2,1)S(1)}, bf16[8,128,1024]{1,2,0:T(8,128)(2,1)}, u32[]{:S(2)}) copy-start(bf16[8,128,1024]{1,2,0:T(8,128)(2,1)} %copy.119) | copy-start | bytes 6291460
  68.6 8.9 copy-start.27
  68.6 9.5 %copy-start.30 = (f32[16,49]{1,0:T(8,128)S(1)}, f32[16,49]{1,0:T(8,128)}, u32[]{:S(2)}) copy-start(f32[16,49]{1,0:T(8,128)} %param.14) | copy-start | bytes 9412
  72.3 9.8 %collective-permute-start.3 = (bf16[14,1024,3]{1,0,2:T(8,128)(2,1)S(1)}, bf16[14,1024,3]{1,0,2:T(8,128)(2,1)S(1)}, u32[]{:S(2)}, u32[]{:S(2)}) collective-permute-start(bf16[14,1024,3]{1,0,2:T(8,128)(2,1)S(1)} %copy.121), channel_id=1, source_target_pairs={{1,0},{2,1},{3,2},{5,4},{6,5},{7,6},{9,8},{10,9},{11,10},{13,12},{... | collective-permute-start | bytes 258056 | tf_op jit(solution)/shard_map/ppermute | solution.py:18
  73.6 4.6 collective-permute-start.2
  85.2 8.4 copy-start.3
  93.6 20.2 %copy-start.2 = (bf16[14,1024,134]{2,1,0:T(8,128)(2,1)}, bf16[14,1024,134]{2,1,0:T(8,128)(2,1)S(1)}, u32[]{:S(2)}) copy-start(bf16[14,1024,134]{2,1,0:T(8,128)(2,1)S(1)} %pad_maximum_fusion) | copy-start | bytes 11526148
  125.6 13.9 %copy-start.26 = (f32[8,16,128]{2,1,0:T(8,128)S(1)}, f32[8,16,128]{2,1,0:T(8,128)}, u32[]{:S(2)}) copy-start(f32[8,16,128]{2,1,0:T(8,128)} %get-tuple-element.35) | copy-start | bytes 196612
  125.6 13.9 %copy-start.25 = (f32[8,16,128]{2,1,0:T(8,128)S(1)}, f32[8,16,128]{2,1,0:T(8,128)}, u32[]{:S(2)}) copy-start(f32[8,16,128]{2,1,0:T(8,128)} %get-tuple-element.34) | copy-start | bytes 196612
  125.6 13.9 %copy-start.24 = (f32[8,16,128]{2,1,0:T(8,128)S(1)}, f32[8,16,128]{2,1,0:T(8,128)}, u32[]{:S(2)}) copy-start(f32[8,16,128]{2,1,0:T(8,128)} %get-tuple-element.33) | copy-start | bytes 196612
  125.6 13.9 %copy-start.23 = (f32[8,16,128]{2,1,0:T(8,128)S(1)}, f32[8,16,128]{2,1,0:T(8,128)}, u32[]{:S(2)}) copy-start(f32[8,16,128]{2,1,0:T(8,128)} %get-tuple-element.32) | copy-start | bytes 196612
  125.6 14.0 %copy-start.22 = (f32[8,16,128]{2,1,0:T(8,128)S(1)}, f32[8,16,128]{2,1,0:T(8,128)}, u32[]{:S(2)}) copy-start(f32[8,16,128]{2,1,0:T(8,128)} %get-tuple-element.31) | copy-start | bytes 196612
  125.6 14.0 %copy-start.21 = (f32[8,16,128]{2,1,0:T(8,128)S(1)}, f32[8,16,128]{2,1,0:T(8,128)}, u32[]{:S(2)}) copy-start(f32[8,16,128]{2,1,0:T(8,128)} %get-tuple-element.30) | copy-start | bytes 196612
  125.6 14.0 %copy-start.20 = (f32[8,16,128]{2,1,0:T(8,128)S(1)}, f32[8,16,128]{2,1,0:T(8,128)}, u32[]{:S(2)}) copy-start(f32[8,16,128]{2,1,0:T(8,128)} %get-tuple-element.29) | copy-start | bytes 196612
  125.6 14.0 %copy-start.19 = (f32[8,16,128]{2,1,0:T(8,128)S(1)}, f32[8,16,128]{2,1,0:T(8,128)}, u32[]{:S(2)}) copy-start(f32[8,16,128]{2,1,0:T(8,128)} %get-tuple-element.28) | copy-start | bytes 196612
  125.6 14.0 %copy-start.18 = (f32[8,16,128]{2,1,0:T(8,128)S(1)}, f32[8,16,128]{2,1,0:T(8,128)}, u32[]{:S(2)}) copy-start(f32[8,16,128]{2,1,0:T(8,128)} %get-tuple-element.27) | copy-start | bytes 196612
  125.6 14.0 %copy-start.17 = (f32[8,16,128]{2,1,0:T(8,128)S(1)}, f32[8,16,128]{2,1,0:T(8,128)}, u32[]{:S(2)}) copy-start(f32[8,16,128]{2,1,0:T(8,128)} %get-tuple-element.26) | copy-start | bytes 196612
  125.6 14.0 %copy-start.16 = (f32[8,16,128]{2,1,0:T(8,128)S(1)}, f32[8,16,128]{2,1,0:T(8,128)}, u32[]{:S(2)}) copy-start(f32[8,16,128]{2,1,0:T(8,128)} %get-tuple-element.25) | copy-start | bytes 196612
  125.7 14.1 %copy-start.15 = (f32[8,16,128]{2,1,0:T(8,128)S(1)}, f32[8,16,128]{2,1,0:T(8,128)}, u32[]{:S(2)}) copy-start(f32[8,16,128]{2,1,0:T(8,128)} %get-tuple-element.24) | copy-start | bytes 196612
  125.7 14.1 %copy-start.14 = (f32[8,16,128]{2,1,0:T(8,128)S(1)}, f32[8,16,128]{2,1,0:T(8,128)}, u32[]{:S(2)}) copy-start(f32[8,16,128]{2,1,0:T(8,128)} %get-tuple-element.23) | copy-start | bytes 196612
  125.7 14.1 %copy-start.13 = (f32[8,16,128]{2,1,0:T(8,128)S(1)}, f32[8,16,128]{2,1,0:T(8,128)}, u32[]{:S(2)}) copy-start(f32[8,16,128]{2,1,0:T(8,128)} %get-tuple-element.22) | copy-start | bytes 196612
  125.7 14.1 %copy-start.12 = (f32[8,16,128]{2,1,0:T(8,128)S(1)}, f32[8,16,128]{2,1,0:T(8,128)}, u32[]{:S(2)}) copy-start(f32[8,16,128]{2,1,0:T(8,128)} %get-tuple-element.21) | copy-start | bytes 196612
  125.7 14.1 %copy-start.11 = (f32[8,16,128]{2,1,0:T(8,128)S(1)}, f32[8,16,128]{2,1,0:T(8,128)}, u32[]{:S(2)}) copy-start(f32[8,16,128]{2,1,0:T(8,128)} %get-tuple-element.20) | copy-start | bytes 196612
  125.7 14.1 %copy-start.10 = (f32[8,16,128]{2,1,0:T(8,128)S(1)}, f32[8,16,128]{2,1,0:T(8,128)}, u32[]{:S(2)}) copy-start(f32[8,16,128]{2,1,0:T(8,128)} %get-tuple-element.19) | copy-start | bytes 196612
  126.7 13.1 %copy-start.9 = (f32[8,16,128]{2,1,0:T(8,128)S(1)}, f32[8,16,128]{2,1,0:T(8,128)}, u32[]{:S(2)}) copy-start(f32[8,16,128]{2,1,0:T(8,128)} %get-tuple-element.18) | copy-start | bytes 196612
  127.6 12.3 %copy-start.8 = (f32[8,16,128]{2,1,0:T(8,128)S(1)}, f32[8,16,128]{2,1,0:T(8,128)}, u32[]{:S(2)}) copy-start(f32[8,16,128]{2,1,0:T(8,128)} %get-tuple-element.17) | copy-start | bytes 196612
  189.2 2.0 copy-start.34
  191.2 1.4 copy-start.35
  192.6 22.8 %copy-start.32 = (bf16[2048,512]{1,0:T(8,128)(2,1)S(1)}, bf16[2048,512]{1,0:T(8,128)(2,1)}, u32[]{:S(2)}) copy-start(bf16[2048,512]{1,0:T(8,128)(2,1)} %param.18) | copy-start | bytes 6291460
  213.5 1.9 copy-start.36
  227.6 3.1 copy-start.29
  236.4 1.9 copy-start.28
  251.9 6.9 copy-start.6
  263.3 621.5 %all-reduce.7.cloned.1.call-start = ((), (), s32[]{:S(2)}) async-start(), calls=%async_computation.1 | async-start | bytes 25165824 | tf_op jit(solution)/shard_map/psum | solution.py:129
  888.7 10.9 %copy-start.1 = (bf16[512,2048]{1,0:T(8,128)(2,1)S(1)}, bf16[512,2048]{1,0:T(8,128)(2,1)}, u32[]{:S(2)}) copy-start(bf16[512,2048]{1,0:T(8,128)(2,1)} %param.17) | copy-start | bytes 6291460
Sparse Core Ops, SparseCore 0:
  263.5 398.8 all-reduce.4
  665.0 219.7 all-reduce.6
